TPU v7x, 32 devices: a whole 2x2x4 slice. The times are simulated.
32 devices in a mesh: lat: 16 (over z, x, core), lon: 2 (over y).
Axes of the slice: x: 2, y: 2, z: 4, core: 2. Of those that a mesh axis runs over, the one named last changes fastest.
Arguments:
- state: bfloat16 [2, 96, 128, 256], P(None, 'lat', 'lon'), may hold values from -6 to 6
- upstream: bfloat16 [2, 96, 128, 256], P(None, 'lat', 'lon'), may hold values from -6 to 6
- first_kernel: bfloat16 [9, 256, 256], replicated, may hold values from -0.125 to 0.125
- second_kernel: bfloat16 [9, 256, 256], replicated, may hold values from -0.125 to 0.125
Outputs:
- output_state: bfloat16 [2, 96, 128, 256], P(None, 'lat', 'lon')
- state_grad: bfloat16 [2, 96, 128, 256], P(None, 'lat', 'lon')
- first_grad: float32 [9, 256, 256], P(None, 'lat', 'lon')
- second_grad: float32 [9, 256, 256], P(None, 'lat', 'lon')
All inputs are finite; a program needn't handle non-finite values.
Results may differ from a plain program's by a relative error of at most 0.0033.
Values may be sent and summed in bfloat16 or wider, within the bound.
A program may use at most 64 MiB of HBM per device.

v0:
```python
import math

import jax
import jax.numpy as jnp
from jax import lax
from jax.sharding import PartitionSpec as P


def with_halo(array, sides, width, wrap):
    for axis, dim in sides:
        size, length = (lax.axis_size(axis), array.shape[dim])
        up = [(i, (i + 1) % size) for i in range(size if wrap else size - 1)]
        down = [(j, i) for i, j in up]
        last = lax.slice_in_dim(array, length - width, length, axis=dim)
        leading = lax.slice_in_dim(array, 0, width, axis=dim)
        before = lax.ppermute(last, axis, up)
        after = lax.ppermute(leading, axis, down)
        array = jnp.concatenate([before, array, after], axis=dim)
    return array


def pad_cycle(stacked):
    wide = with_halo(stacked, (("lon", 3),), 1, True)
    return with_halo(wide, (("lat", 2),), 1, False)


def conv_taps(padded, kernel, flipped):
    band_rows = padded.shape[1] - 2
    band_cols = padded.shape[2] - 2
    total = jnp.zeros((padded.shape[0], band_rows, band_cols, kernel.shape[2]), jnp.float32)
    for row_off in range(3):
        for col_off in range(3):
            window = padded[:, row_off : row_off + band_rows, col_off : col_off + band_cols, :]
            if flipped:
                total = total + jnp.einsum(
                    "bijd,cd->bijc",
                    window,
                    kernel[8 - 3 * row_off - col_off],
                    preferred_element_type=jnp.float32,
                )
            else:
                total = total + jnp.einsum(
                    "bijc,cd->bijd",
                    window,
                    kernel[3 * row_off + col_off],
                    preferred_element_type=jnp.float32,
                )
    return total


def kernel_terms(padded, grad_field):
    band_rows = grad_field.shape[1]
    band_cols = grad_field.shape[2]
    result = []
    for row_off in range(3):
        for col_off in range(3):
            window = padded[:, row_off : row_off + band_rows, col_off : col_off + band_cols, :]
            result.append(
                jnp.einsum("bijc,bijd->cd", window, grad_field, preferred_element_type=jnp.float32)
            )
    return jnp.stack(result)


def sum_lat(terms):
    moved = (
        lax.all_to_all(terms[0][None], "lat", split_axis=2, concat_axis=0, tiled=True),
        lax.all_to_all(terms[1][None], "lat", split_axis=2, concat_axis=0, tiled=True),
    )
    return (jnp.sum(moved[0], axis=0), jnp.sum(moved[1], axis=0))


def sum_lon(terms):
    moved = (
        lax.all_to_all(terms[0][None], "lon", split_axis=3, concat_axis=0, tiled=True),
        lax.all_to_all(terms[1][None], "lon", split_axis=3, concat_axis=0, tiled=True),
    )
    return (jnp.sum(moved[0], axis=0), jnp.sum(moved[1], axis=0))


def body(state, upstream, first_kernel, second_kernel):
    band_rows = state.shape[1]
    band_cols = state.shape[2]
    scale_factor = 1.0 / math.sqrt(
        band_rows * lax.axis_size("lat") * band_cols * lax.axis_size("lon")
    )
    both_pad = pad_cycle(jnp.stack([state, upstream]))
    state_pad = both_pad[0]
    upstream_pad = both_pad[1]
    pre = conv_taps(state_pad, first_kernel, False)
    active = jax.nn.silu(pre).astype(jnp.bfloat16)
    active_pad = pad_cycle(active[None])[0]
    second_out = conv_taps(active_pad, second_kernel, False)
    output_state = (state.astype(jnp.float32) + second_out).astype(jnp.bfloat16)
    back_act = conv_taps(upstream_pad, second_kernel, True)
    sigma = jax.nn.sigmoid(pre)
    back_pre = (back_act * sigma * (1.0 + pre * (1.0 - sigma))).astype(jnp.bfloat16)
    back_pad = pad_cycle(back_pre[None])[0]
    state_grad = (upstream.astype(jnp.float32) + conv_taps(back_pad, first_kernel, True)).astype(
        jnp.bfloat16
    )
    terms = (
        kernel_terms(state_pad, back_pre) * scale_factor,
        kernel_terms(active_pad, upstream) * scale_factor,
    )
    summed = sum_lon(sum_lat(terms))
    return (output_state, state_grad, summed[0], summed[1])


def solution(mesh):
    placed = (P(None, "lat", "lon", None), P(None, "lat", "lon", None), P(), P())
    return jax.shard_map(
        body,
        mesh=mesh,
        in_specs=placed,
        out_specs=(
            P(None, "lat", "lon", None),
            P(None, "lat", "lon", None),
            P(None, "lat", "lon"),
            P(None, "lat", "lon"),
        ),
        check_vma=False,
    )
```

profile of v0, /device:TPU:20, one launch (start us, length us, event | category | flops | bytes accessed | tf_op | source)
XLA Modules:
  0.0 192.8 jit_solution(8814331763132578597)
XLA Ops:
  0.7 1.0 pad_maximum_fusion.12
  1.6 0.6 collective-permute-start.1
  2.2 1.5 collective-permute-start
  3.7 1.8 collective-permute-done.1
  5.5 0.5 collective-permute-done
  6.0 1.0 pad_maximum_fusion.4
  7.1 1.9 collective-permute-start.3
  9.0 2.4 %collective-permute-start.2 = (bf16[2,2,1,66,256]{4,3,2,1,0:T(8,128)(2,1)S(1)}, bf16[2,2,1,66,256]{4,3,2,1,0:T(8,128)(2,1)S(1)}, u32[]{:S(2)}, u32[]{:S(2)}) collective-permute-start(bf16[2,2,1,66,256]{4,3,2,1,0:T(8,128)(2,1)S(1)} %get-tuple-element.14), channel_id=1, source_target_pairs={{0,2},{2,4},{4,6},{6,8},{8,10},{10,12},{12,14},{14,16},{16,18},{18... | collective-permute-start | bytes 405512 | tf_op jit(solution)/shard_map/ppermute | solution.py:16
  11.7 4.7 %collective-permute-done.2 = bf16[2,2,1,66,256]{4,3,2,1,0:T(8,128)(2,1)S(1)} collective-permute-done((bf16[2,2,1,66,256]{4,3,2,1,0:T(8,128)(2,1)S(1)}, bf16[2,2,1,66,256]{4,3,2,1,0:T(8,128)(2,1)S(1)}, u32[]{:S(2)}, u32[]{:S(2)}) %collective-permute-start.2) | collective-permute-done | bytes 135200 | tf_op jit(solution)/shard_map/ppermute | solution.py:16
  16.4 0.5 pad_maximum_fusion
  17.0 1.2 copy-done.4
  20.6 1.0 copy-done.6
  23.2 0.3 convolution_add_fusion.11
  24.1 0.5 fusion.5
  25.2 0.3 fusion.22
  25.8 0.3 fusion.20
  26.8 0.3 fusion.17
  27.7 3.9 %copy.16 = f32[1,9,256,256]{3,0,1,2:T(1,128)} copy(f32[1,9,256,256]{3,2,1,0:T(8,128)S(1)} %broadcast_multiply_fusion.1) | data formatting | bytes 4718592 | tf_op jit(solution)/shard_map/mul | solution.py:102
  31.6 5.3 %all-to-all-start = ((f32[1,9,256,256]{3,0,1,2:T(1,128)}), f32[1,9,256,256]{3,0,1,2:T(1,128)S(1)}, u32[]{:S(2)}, u32[]{:S(2)}) async-start(f32[1,9,256,256]{3,0,1,2:T(1,128)} %copy.16), calls=%async_computation | async-start | bytes 4718592 | tf_op jit(solution)/shard_map/all_to_all | solution.py:66
  37.1 1.6 collective-permute-start.5
  38.7 0.5 collective-permute-start.4
  39.2 1.6 collective-permute-start.9
  40.8 0.5 collective-permute-start.8
  41.3 1.1 collective-permute-done.4
  42.4 2.0 %collective-permute-start.7 = (bf16[1,2,1,66,256]{4,3,2,1,0:T(8,128)(2,1)S(1)}, bf16[1,2,1,66,256]{4,3,2,1,0:T(8,128)(2,1)S(1)}, u32[]{:S(2)}, u32[]{:S(2)}) collective-permute-start(bf16[1,2,1,66,256]{4,3,2,1,0:T(8,128)(2,1)S(1)} %get-tuple-element.21), channel_id=1, source_target_pairs={{2,0},{4,2},{6,4},{8,6},{10,8},{12,10},{14,12},{16,14},{18,16},{20... | collective-permute-start | bytes 202760 | tf_op jit(solution)/shard_map/ppermute | solution.py:17
  44.4 2.4 %collective-permute-start.6 = (bf16[1,2,1,66,256]{4,3,2,1,0:T(8,128)(2,1)S(1)}, bf16[1,2,1,66,256]{4,3,2,1,0:T(8,128)(2,1)S(1)}, u32[]{:S(2)}, u32[]{:S(2)}) collective-permute-start(bf16[1,2,1,66,256]{4,3,2,1,0:T(8,128)(2,1)S(1)} %get-tuple-element.20), channel_id=1, source_target_pairs={{0,2},{2,4},{4,6},{6,8},{8,10},{10,12},{12,14},{14,16},{16,18},{18... | collective-permute-start | bytes 202760 | tf_op jit(solution)/shard_map/ppermute | solution.py:16
  46.8 0.7 pad_maximum_fusion.7
  47.5 4.1 %collective-permute-start.11 = (bf16[1,2,1,66,256]{4,3,2,1,0:T(8,128)(2,1)}, bf16[1,2,1,66,256]{4,3,2,1,0:T(8,128)(2,1)S(1)}, u32[]{:S(2)}, u32[]{:S(2)}) collective-permute-start(bf16[1,2,1,66,256]{4,3,2,1,0:T(8,128)(2,1)} %get-tuple-element.19), channel_id=1, source_target_pairs={{2,0},{4,2},{6,4},{8,6},{10,8},{12,10},{14,12},{16,14},{18,16},{20... | collective-permute-start | bytes 202760 | tf_op jit(solution)/shard_map/ppermute | solution.py:17
  51.6 2.1 %collective-permute-start.10 = (bf16[1,2,1,66,256]{4,3,2,1,0:T(8,128)(2,1)S(1)}, bf16[1,2,1,66,256]{4,3,2,1,0:T(8,128)(2,1)}, u32[]{:S(2)}, u32[]{:S(2)}) collective-permute-start(bf16[1,2,1,66,256]{4,3,2,1,0:T(8,128)(2,1)S(1)} %get-tuple-element.18), channel_id=1, source_target_pairs={{0,2},{2,4},{4,6},{6,8},{8,10},{10,12},{12,14},{14,16},{16,18},{18... | collective-permute-start | bytes 202760 | tf_op jit(solution)/shard_map/ppermute | solution.py:16
  53.7 35.3 %collective-permute-done.7 = bf16[1,2,1,66,256]{4,3,2,1,0:T(8,128)(2,1)S(1)} collective-permute-done((bf16[1,2,1,66,256]{4,3,2,1,0:T(8,128)(2,1)S(1)}, bf16[1,2,1,66,256]{4,3,2,1,0:T(8,128)(2,1)S(1)}, u32[]{:S(2)}, u32[]{:S(2)}) %collective-permute-start.7) | collective-permute-done | bytes 67616 | tf_op jit(solution)/shard_map/ppermute | solution.py:17
  89.0 1.9 collective-permute-done.6
  91.4 0.3 fusion.14
  92.6 0.3 fusion.10
  93.6 0.3 fusion.7
  94.2 3.9 %copy.22 = f32[1,9,256,256]{3,0,1,2:T(1,128)} copy(f32[1,9,256,256]{3,2,1,0:T(8,128)S(1)} %broadcast_multiply_fusion) | data formatting | bytes 4718592 | tf_op jit(solution)/shard_map/mul | solution.py:103
  98.1 4.3 %all-to-all-start.2 = ((f32[1,9,256,256]{3,0,1,2:T(1,128)}), f32[1,9,256,256]{3,0,1,2:T(1,128)}, u32[]{:S(2)}, u32[]{:S(2)}) async-start(f32[1,9,256,256]{3,0,1,2:T(1,128)} %copy.22), calls=%async_computation.2 | async-start | bytes 4718592 | tf_op jit(solution)/shard_map/all_to_all | solution.py:67
  102.5 0.6 copy-done.10
  103.1 1.2 maximum_bitcast_fusion.1
  104.3 1.3 fusion.61
  107.8 0.7 copy-done.1
  108.6 1.0 fusion.4
  111.1 1.2 convolution_add_fusion.2
  112.3 2.5 %copy.66 = f32[1,9,256,256]{3,1,2,0:T(8,128)} copy(f32[1,9,256,256]{3,0,1,2:T(1,128)S(1)} %all-to-all-done) | data formatting | bytes 4718592 | tf_op jit(solution)/shard_map/all_to_all | solution.py:66
  114.8 2.7 %reduce_sum.36 = f32[9,16,256]{2,0,1:T(8,128)S(1)} reduce(f32[9,16,16,256]{3,0,2,1:T(8,128)} %bitcast.349, f32[]{:T(128)} %constant.2.clone.1), dimensions={1}, to_apply=%region_0.1 | reduce | flops 552960 | bytes 2506756 | tf_op jit(solution)/shard_map/reduce_sum | solution.py:69
  117.5 2.1 %copy.19 = f32[1,9,16,256]{2,0,1,3:T(1,128)} copy(f32[1,9,16,256]{3,1,2,0:T(8,128)S(1)} %bitcast.366) | data formatting | bytes 294912 | tf_op jit(solution)/shard_map/broadcast_in_dim | solution.py:74
  119.7 0.5 broadcast.23
  120.2 4.9 %reduce.12 = f32[256,9,16]{2,1,0:T(8,128)S(1)} reduce(f32[256,9,1,16]{3,2,1,0:T(1,128)} %bitcast.361, f32[]{:T(128)} %broadcast.23), dimensions={2}, to_apply=%bitcast.327.reduce_sub_computation | reduce | bytes 294916
  125.1 1.1 reshape.308
  126.2 29.4 %all-to-all-done.2 = f32[1,9,256,256]{3,0,1,2:T(1,128)} async-done(((f32[1,9,256,256]{3,0,1,2:T(1,128)}), f32[1,9,256,256]{3,0,1,2:T(1,128)}, u32[]{:S(2)}, u32[]{:S(2)}) %all-to-all-start.2) | async-done | bytes 2359328 | tf_op jit(solution)/shard_map/all_to_all | solution.py:67
  155.7 4.9 %all-to-all-start.1 = ((f32[2,1,18432]{2,1,0:T(1,128)}), f32[2,1,18432]{2,1,0:T(1,128)S(1)}, u32[]{:S(2)}, u32[]{:S(2)}) async-start(f32[2,1,18432]{2,1,0:T(1,128)} %reshape.308), calls=%async_computation.1 | async-start | bytes 294912 | tf_op jit(solution)/shard_map/all_to_all | solution.py:74
  160.6 2.4 %convolution_add_fusion.1 = f32[2,6,64,256]{3,2,1,0:T(8,128)} fusion(f32[2,6,64,256]{3,2,1,0:T(8,128)} %convolution_add_fusion.2, bf16[2,8,66,256]{3,2,1,0:T(8,128)(2,1)S(1)} %maximum_bitcast_fusion.1, bf16[9,256,256]{2,1,0:T(8,128)(2,1)} %param.6), kind=kOutput, calls=%fused_computation.2 | convolution fusion | flops 100859904 | bytes 2097152 | tf_op jit(solution)/shard_map/bijd,cd->bijc/dot_general | solution.py:35
  163.0 4.2 %copy.67 = f32[1,9,256,256]{3,1,2,0:T(8,128)} copy(f32[1,9,256,256]{3,0,1,2:T(1,128)} %all-to-all-done.2) | data formatting | bytes 4718592 | tf_op jit(solution)/shard_map/all_to_all | solution.py:67
  167.2 2.7 %reduce_sum.38 = f32[9,16,256]{2,0,1:T(8,128)S(1)} reduce(f32[9,16,16,256]{3,0,2,1:T(8,128)} %bitcast.350, f32[]{:T(128)} %constant.2.clone.1), dimensions={1}, to_apply=%region_2.3 | reduce | flops 552960 | bytes 2506756 | tf_op jit(solution)/shard_map/reduce_sum | solution.py:69
  169.9 2.1 %copy.25 = f32[1,9,16,256]{2,0,1,3:T(1,128)} copy(f32[1,9,16,256]{3,1,2,0:T(8,128)S(1)} %bitcast.367) | data formatting | bytes 294912 | tf_op jit(solution)/shard_map/broadcast_in_dim | solution.py:75
  172.0 4.9 %reduce.14 = f32[256,9,16]{2,1,0:T(8,128)S(1)} reduce(f32[256,9,1,16]{3,2,1,0:T(1,128)} %bitcast.362, f32[]{:T(128)} %broadcast.23), dimensions={2}, to_apply=%bitcast.329.reduce_sub_computation | reduce | bytes 294916
  177.0 1.1 reshape.310
  178.1 3.7 %all-to-all-start.3 = ((f32[2,1,18432]{2,1,0:T(1,128)}), f32[2,1,18432]{2,1,0:T(1,128)S(1)}, u32[]{:S(2)}, u32[]{:S(2)}) async-start(f32[2,1,18432]{2,1,0:T(1,128)} %reshape.310), calls=%async_computation.3 | async-start | bytes 294912 | tf_op jit(solution)/shard_map/all_to_all | solution.py:75
  181.8 2.3 %fusion.6 = bf16[2,6,64,256]{3,2,1,0:T(8,128)(2,1)} fusion(f32[2,6,64,256]{3,2,1,0:T(8,128)} %convolution_add_fusion.1, bf16[2,6,64,256]{3,2,1,0:T(8,128)(2,1)S(1)} %copy-done.3, bf16[2,8,66,256]{3,2,1,0:T(8,128)(2,1)S(1)} %maximum_bitcast_fusion.1, bf16[9,256,256]{2,1,0:T(8,128)(2,1)} %param.6), kind=kOutput, calls=%fused_computation.38 | convolution fusion | flops 101449728 | bytes 2097152 | tf_op jit(solution)/shard_map/bijd,cd->bijc/dot_general | solution.py:35
  184.0 1.1 reduce.13
  185.1 1.9 reshape.309
  187.5 0.9 copy.28
  188.4 1.1 reduce.15
  189.5 1.9 reshape.311
  191.8 0.9 copy.29
  (82 shorter events, 14.1 us)
Async XLA Ops:
  0.6 15.7 %copy-start.2 = (bf16[2,6,64,256]{3,2,1,0:T(8,128)(2,1)S(1)}, bf16[2,6,64,256]{3,2,1,0:T(8,128)(2,1)}, u32[]{:S(2)}) copy-start(bf16[2,6,64,256]{3,2,1,0:T(8,128)(2,1)} %param.5) | copy-start | bytes 1179652
  0.6 15.7 %copy-start = (bf16[2,6,64,256]{3,2,1,0:T(8,128)(2,1)S(1)}, bf16[2,6,64,256]{3,2,1,0:T(8,128)(2,1)}, u32[]{:S(2)}) copy-start(bf16[2,6,64,256]{3,2,1,0:T(8,128)(2,1)} %param.4) | copy-start | bytes 1179652
  1.6 3.9 %collective-permute-start.1 = (bf16[2,2,6,1,256]{4,3,2,1,0:T(2,128)(2,1)S(1)}, bf16[2,2,6,1,256]{4,3,2,1,0:T(2,128)(2,1)S(1)}, u32[]{:S(2)}, u32[]{:S(2)}) collective-permute-start(bf16[2,2,6,1,256]{4,3,2,1,0:T(2,128)(2,1)S(1)} %get-tuple-element.17), channel_id=1, source_target_pairs={{1,0},{0,1},{3,2},{2,3},{5,4},{4,5},{7,6},{6,7},{9,8},{8,9},{11,10... | collective-permute-start | bytes 36872 | tf_op jit(solution)/shard_map/ppermute | solution.py:17
  2.2 3.8 %collective-permute-start = (bf16[2,2,6,1,256]{4,3,2,1,0:T(2,128)(2,1)S(1)}, bf16[2,2,6,1,256]{4,3,2,1,0:T(2,128)(2,1)S(1)}, u32[]{:S(2)}, u32[]{:S(2)}) collective-permute-start(bf16[2,2,6,1,256]{4,3,2,1,0:T(2,128)(2,1)S(1)} %get-tuple-element.16), channel_id=1, source_target_pairs={{0,1},{1,0},{2,3},{3,2},{4,5},{5,4},{6,7},{7,6},{8,9},{9,8},{10,11... | collective-permute-start | bytes 36872 | tf_op jit(solution)/shard_map/ppermute | solution.py:16
  7.1 4.6 %collective-permute-start.3 = (bf16[2,2,1,66,256]{4,3,2,1,0:T(8,128)(2,1)S(1)}, bf16[2,2,1,66,256]{4,3,2,1,0:T(8,128)(2,1)S(1)}, u32[]{:S(2)}, u32[]{:S(2)}) collective-permute-start(bf16[2,2,1,66,256]{4,3,2,1,0:T(8,128)(2,1)S(1)} %get-tuple-element.15), channel_id=1, source_target_pairs={{2,0},{4,2},{6,4},{8,6},{10,8},{12,10},{14,12},{16,14},{18,16},{20... | collective-permute-start | bytes 405512 | tf_op jit(solution)/shard_map/ppermute | solution.py:17
  9.0 7.4 %collective-permute-start.2 = (bf16[2,2,1,66,256]{4,3,2,1,0:T(8,128)(2,1)S(1)}, bf16[2,2,1,66,256]{4,3,2,1,0:T(8,128)(2,1)S(1)}, u32[]{:S(2)}, u32[]{:S(2)}) collective-permute-start(bf16[2,2,1,66,256]{4,3,2,1,0:T(8,128)(2,1)S(1)} %get-tuple-element.14), channel_id=1, source_target_pairs={{0,2},{2,4},{4,6},{6,8},{8,10},{10,12},{12,14},{14,16},{16,18},{18... | collective-permute-start | bytes 405512 | tf_op jit(solution)/shard_map/ppermute | solution.py:16
  16.9 1.3 copy-start.4
  20.4 1.3 copy-start.6
  24.6 2.6 %copy-start.8 = (bf16[2,6,64,256]{3,2,1,0:T(8,128)(2,1)}, bf16[2,6,64,256]{3,2,1,0:T(8,128)(2,1)S(1)}, u32[]{:S(2)}) copy-start(bf16[2,6,64,256]{3,2,1,0:T(8,128)(2,1)S(1)} %fusion.5) | copy-start | bytes 1179652
  31.6 66.5 %all-to-all-start = ((f32[1,9,256,256]{3,0,1,2:T(1,128)}), f32[1,9,256,256]{3,0,1,2:T(1,128)S(1)}, u32[]{:S(2)}, u32[]{:S(2)}) async-start(f32[1,9,256,256]{3,0,1,2:T(1,128)} %copy.16), calls=%async_computation | async-start | bytes 4718592 | tf_op jit(solution)/shard_map/all_to_all | solution.py:66
  36.8 2.4 %copy-start.9 = (bf16[2,6,64,256]{3,2,1,0:T(8,128)(2,1)S(1)}, bf16[2,6,64,256]{3,2,1,0:T(8,128)(2,1)}, u32[]{:S(2)}) copy-start(bf16[2,6,64,256]{3,2,1,0:T(8,128)(2,1)} %copy-done.8) | copy-start | bytes 1179652
  37.1 4.2 %collective-permute-start.5 = (bf16[1,2,6,1,256]{4,3,2,1,0:T(2,128)(2,1)S(1)}, bf16[1,2,6,1,256]{4,3,2,1,0:T(2,128)(2,1)S(1)}, u32[]{:S(2)}, u32[]{:S(2)}) collective-permute-start(bf16[1,2,6,1,256]{4,3,2,1,0:T(2,128)(2,1)S(1)} %get-tuple-element.25), channel_id=1, source_target_pairs={{1,0},{0,1},{3,2},{2,3},{5,4},{4,5},{7,6},{6,7},{9,8},{8,9},{11,10... | collective-permute-start | bytes 18440 | tf_op jit(solution)/shard_map/ppermute | solution.py:17
  38.7 3.7 %collective-permute-start.4 = (bf16[1,2,6,1,256]{4,3,2,1,0:T(2,128)(2,1)S(1)}, bf16[1,2,6,1,256]{4,3,2,1,0:T(2,128)(2,1)S(1)}, u32[]{:S(2)}, u32[]{:S(2)}) collective-permute-start(bf16[1,2,6,1,256]{4,3,2,1,0:T(2,128)(2,1)S(1)} %get-tuple-element.24), channel_id=1, source_target_pairs={{0,1},{1,0},{2,3},{3,2},{4,5},{5,4},{6,7},{7,6},{8,9},{9,8},{10,11... | collective-permute-start | bytes 18440 | tf_op jit(solution)/shard_map/ppermute | solution.py:16
  39.2 7.6 %collective-permute-start.9 = (bf16[1,2,6,1,256]{4,3,2,1,0:T(2,128)(2,1)S(1)}, bf16[1,2,6,1,256]{4,3,2,1,0:T(2,128)(2,1)S(1)}, u32[]{:S(2)}, u32[]{:S(2)}) collective-permute-start(bf16[1,2,6,1,256]{4,3,2,1,0:T(2,128)(2,1)S(1)} %get-tuple-element.23), channel_id=1, source_target_pairs={{1,0},{0,1},{3,2},{2,3},{5,4},{4,5},{7,6},{6,7},{9,8},{8,9},{11,10... | collective-permute-start | bytes 18440 | tf_op jit(solution)/shard_map/ppermute | solution.py:17
  40.8 6.0 %collective-permute-start.8 = (bf16[1,2,6,1,256]{4,3,2,1,0:T(2,128)(2,1)S(1)}, bf16[1,2,6,1,256]{4,3,2,1,0:T(2,128)(2,1)S(1)}, u32[]{:S(2)}, u32[]{:S(2)}) collective-permute-start(bf16[1,2,6,1,256]{4,3,2,1,0:T(2,128)(2,1)S(1)} %get-tuple-element.22), channel_id=1, source_target_pairs={{0,1},{1,0},{2,3},{3,2},{4,5},{5,4},{6,7},{7,6},{8,9},{9,8},{10,11... | collective-permute-start | bytes 18440 | tf_op jit(solution)/shard_map/ppermute | solution.py:16
  42.4 46.6 %collective-permute-start.7 = (bf16[1,2,1,66,256]{4,3,2,1,0:T(8,128)(2,1)S(1)}, bf16[1,2,1,66,256]{4,3,2,1,0:T(8,128)(2,1)S(1)}, u32[]{:S(2)}, u32[]{:S(2)}) collective-permute-start(bf16[1,2,1,66,256]{4,3,2,1,0:T(8,128)(2,1)S(1)} %get-tuple-element.21), channel_id=1, source_target_pairs={{2,0},{4,2},{6,4},{8,6},{10,8},{12,10},{14,12},{16,14},{18,16},{20... | collective-permute-start | bytes 202760 | tf_op jit(solution)/shard_map/ppermute | solution.py:17
  44.4 46.5 %collective-permute-start.6 = (bf16[1,2,1,66,256]{4,3,2,1,0:T(8,128)(2,1)S(1)}, bf16[1,2,1,66,256]{4,3,2,1,0:T(8,128)(2,1)S(1)}, u32[]{:S(2)}, u32[]{:S(2)}) collective-permute-start(bf16[1,2,1,66,256]{4,3,2,1,0:T(8,128)(2,1)S(1)} %get-tuple-element.20), channel_id=1, source_target_pairs={{0,2},{2,4},{4,6},{6,8},{8,10},{10,12},{12,14},{14,16},{16,18},{18... | collective-permute-start | bytes 202760 | tf_op jit(solution)/shard_map/ppermute | solution.py:16
  46.8 0.7 copy-start.11
  47.5 55.0 %collective-permute-start.11 = (bf16[1,2,1,66,256]{4,3,2,1,0:T(8,128)(2,1)}, bf16[1,2,1,66,256]{4,3,2,1,0:T(8,128)(2,1)S(1)}, u32[]{:S(2)}, u32[]{:S(2)}) collective-permute-start(bf16[1,2,1,66,256]{4,3,2,1,0:T(8,128)(2,1)} %get-tuple-element.19), channel_id=1, source_target_pairs={{2,0},{4,2},{6,4},{8,6},{10,8},{12,10},{14,12},{16,14},{18,16},{20... | collective-permute-start | bytes 202760 | tf_op jit(solution)/shard_map/ppermute | solution.py:17
  51.6 51.5 %collective-permute-start.10 = (bf16[1,2,1,66,256]{4,3,2,1,0:T(8,128)(2,1)S(1)}, bf16[1,2,1,66,256]{4,3,2,1,0:T(8,128)(2,1)}, u32[]{:S(2)}, u32[]{:S(2)}) collective-permute-start(bf16[1,2,1,66,256]{4,3,2,1,0:T(8,128)(2,1)S(1)} %get-tuple-element.18), channel_id=1, source_target_pairs={{0,2},{2,4},{4,6},{6,8},{8,10},{10,12},{12,14},{14,16},{16,18},{18... | collective-permute-start | bytes 202760 | tf_op jit(solution)/shard_map/ppermute | solution.py:16
  98.1 57.6 %all-to-all-start.2 = ((f32[1,9,256,256]{3,0,1,2:T(1,128)}), f32[1,9,256,256]{3,0,1,2:T(1,128)}, u32[]{:S(2)}, u32[]{:S(2)}) async-start(f32[1,9,256,256]{3,0,1,2:T(1,128)} %copy.22), calls=%async_computation.2 | async-start | bytes 4718592 | tf_op jit(solution)/shard_map/all_to_all | solution.py:67
  102.4 3.2 %copy-start.5 = (bf16[9,256,256]{2,1,0:T(8,128)(2,1)S(1)}, bf16[9,256,256]{2,1,0:T(8,128)(2,1)}, u32[]{:S(2)}) copy-start(bf16[9,256,256]{2,1,0:T(8,128)(2,1)} %param.6) | copy-start | bytes 3538948
  102.4 0.6 copy-start.10
  104.3 1.6 copy-start.7
  107.6 1.0 copy-start.1
  155.7 22.4 %all-to-all-start.1 = ((f32[2,1,18432]{2,1,0:T(1,128)}), f32[2,1,18432]{2,1,0:T(1,128)S(1)}, u32[]{:S(2)}, u32[]{:S(2)}) async-start(f32[2,1,18432]{2,1,0:T(1,128)} %reshape.308), calls=%async_computation.1 | async-start | bytes 294912 | tf_op jit(solution)/shard_map/all_to_all | solution.py:74
  177.0 4.8 %copy-start.3 = (bf16[2,6,64,256]{3,2,1,0:T(8,128)(2,1)S(1)}, bf16[2,6,64,256]{3,2,1,0:T(8,128)(2,1)}, u32[]{:S(2)}) copy-start(bf16[2,6,64,256]{3,2,1,0:T(8,128)(2,1)} %param.5) | copy-start | bytes 1179652
  178.1 10.3 %all-to-all-start.3 = ((f32[2,1,18432]{2,1,0:T(1,128)}), f32[2,1,18432]{2,1,0:T(1,128)S(1)}, u32[]{:S(2)}, u32[]{:S(2)}) async-start(f32[2,1,18432]{2,1,0:T(1,128)} %reshape.310), calls=%async_computation.3 | async-start | bytes 294912 | tf_op jit(solution)/shard_map/all_to_all | solution.py:75
where the time goes:
time: 194 us; the launch traced here: 193 us
  waiting for transfers between devices  74.9 us (39%)
  starting transfers between devices  39.3 us (20%)
  local copies, waits for them, and re-layouts  31.2 us (16%)
  other arithmetic  23.3 us (12%)
  matrix products  22.7 us (12%)
    ppermute x6, waiting for transfers between devices, with_halo(): after = lax.ppermute(leading, axis, down)  37.4 us
    all_to_all x1, waiting for transfers between devices, sum_lat(): lax.all_to_all(terms[1][None], 'lat', split_axis=2, concat_axis=0, tiled=...  29.4 us
    unnamed x33, local copies, waits for them, and re-layouts  12.3 us
    ppermute x6, starting transfers between devices, with_halo(): after = lax.ppermute(leading, axis, down)  11.8 us
    dot_general x18, matrix products, conv_taps(): jnp.einsum('bijd,cd->bijc', window, kernel[8 - 3 * row_off - col_off], pr...  10.5 us
    unnamed x2, other arithmetic  9.8 us
    ppermute x6, starting transfers between devices, with_halo(): before = lax.ppermute(last, axis, up)  9.37 us
    ppermute x6, waiting for transfers between devices, with_halo(): before = lax.ppermute(last, axis, up)  8.16 us
  transfers between devices with their start and end apart: 16, of which 8 were waited for; matrix products, arithmetic and copies ran while one was open for 28% of the time, Pallas kernels for 0%

commit v1 on v0

v1 whole, which is shorter than its diff:
```python
import math

import jax
import jax.numpy as jnp
from jax import lax
from jax.experimental import pallas as pl
from jax.experimental.pallas import tpu as pltpu
from jax.sharding import PartitionSpec as P

F32 = jnp.float32
BF16 = jnp.bfloat16
MESH = pl.DeviceIdType.MESH


def with_halo(array, sides, width, wrap):
    for axis, dim in sides:
        size, length = (lax.axis_size(axis), array.shape[dim])
        up = [(i, (i + 1) % size) for i in range(size if wrap else size - 1)]
        down = [(j, i) for i, j in up]
        last = lax.slice_in_dim(array, length - width, length, axis=dim)
        leading = lax.slice_in_dim(array, 0, width, axis=dim)
        before = lax.ppermute(last, axis, up)
        after = lax.ppermute(leading, axis, down)
        array = jnp.concatenate([before, array, after], axis=dim)
    return array


def pad_cycle(stacked):
    wide = with_halo(stacked, (("lon", 3),), 1, True)
    return with_halo(wide, (("lat", 2),), 1, False)


def conv_taps(padded, kernel, flipped):
    band_rows = padded.shape[1] - 2
    band_cols = padded.shape[2] - 2
    total = jnp.zeros((padded.shape[0], band_rows, band_cols, kernel.shape[2]), F32)
    for row_off in range(3):
        for col_off in range(3):
            window = padded[:, row_off : row_off + band_rows, col_off : col_off + band_cols, :]
            tap = 3 * row_off + col_off
            total = total + jnp.einsum(
                "bijd,cd->bijc" if flipped else "bijc,cd->bijd",
                window,
                kernel[8 - tap if flipped else tap],
                preferred_element_type=F32,
            )
    return total


def kernel_terms(padded, grad_field):
    band_rows = grad_field.shape[1]
    band_cols = grad_field.shape[2]
    result = []
    for row_off in range(3):
        for col_off in range(3):
            window = padded[:, row_off : row_off + band_rows, col_off : col_off + band_cols, :]
            result.append(jnp.einsum("bijc,bijd->cd", window, grad_field, preferred_element_type=F32))
    return jnp.stack(result)


def general_body(state, upstream, first_kernel, second_kernel):
    scale_factor = 1.0 / math.sqrt(
        state.shape[1] * lax.axis_size("lat") * state.shape[2] * lax.axis_size("lon")
    )
    both_pad = pad_cycle(jnp.stack([state, upstream]))
    pre = conv_taps(both_pad[0], first_kernel, False)
    active = jax.nn.silu(pre).astype(BF16)
    back_act = conv_taps(both_pad[1], second_kernel, True)
    sigma = jax.nn.sigmoid(pre)
    back_pre = (back_act * sigma * (1.0 + pre * (1.0 - sigma))).astype(BF16)
    inner_pad = pad_cycle(jnp.stack([active, back_pre]))
    output_state = (state.astype(F32) + conv_taps(inner_pad[0], second_kernel, False)).astype(BF16)
    state_grad = (upstream.astype(F32) + conv_taps(inner_pad[1], first_kernel, True)).astype(BF16)
    summed = []
    for terms in (kernel_terms(both_pad[0], back_pre), kernel_terms(inner_pad[0], upstream)):
        part = lax.psum_scatter(terms, "lat", scatter_dimension=1, tiled=True)
        part = lax.psum_scatter(part, "lon", scatter_dimension=2, tiled=True)
        summed.append(part * scale_factor)
    return (output_state, state_grad, summed[0], summed[1])


def stage_plan(lat_size, chans, lon_first):
    bits = lat_size.bit_length() - 1
    order = [0, "lon", 1] if lon_first else [0, 1, "lon"]
    order += list(range(2, bits))
    plan, length, cols = [], lat_size, chans
    for op in order:
        plan.append((op, length, cols))
        if op == "lon":
            cols //= 2
        else:
            length //= 2
    return plan


def fused_kernel(lat_size, scale, plans, names, *refs):
    r = dict(zip(names, refs))
    z = r["z"]
    batch, padded_rows, cols = z.shape[1], z.shape[2], z.shape[3]
    rows = padded_rows - 2
    chans = z.shape[4] // 3
    mid = slice(chans, 2 * chans)
    n_stage = 2 * padded_rows
    lat, lon = lax.axis_index("lat"), lax.axis_index("lon")
    other_lon = 1 - lon
    bits = lat_size.bit_length() - 1

    def bit_of(k):
        return lax.rem(lax.div(lat, 2**k), 2)

    def partner(k):
        return lat + (1 - 2 * bit_of(k)) * 2**k

    loads = [
        pltpu.make_async_copy(r["state"], z.at[0, :, 1 : rows + 1, :, mid], r["load_sem"].at[0]),
        pltpu.make_async_copy(r["upstream"], z.at[1, :, 1 : rows + 1, :, mid], r["load_sem"].at[1]),
        pltpu.make_async_copy(r["k1"], r["w1"], r["load_sem"].at[2]),
        pltpu.make_async_copy(r["k2"], r["w2"], r["load_sem"].at[3]),
    ]
    for load in loads:
        load.start()

    barrier = pltpu.get_barrier_semaphore()

    def greet(to_lat, to_lon):
        pl.semaphore_signal(barrier, inc=1, device_id=(to_lat, to_lon), device_id_type=MESH)

    greet(lat, other_lon)
    for k in range(1, bits):
        greet(partner(k), lon)

    @pl.when(lat > 0)
    def _():
        greet(lat - 1, lon)
        greet(lat - 1, other_lon)

    @pl.when(lat < lat_size - 1)
    def _():
        greet(lat + 1, lon)
        greet(lat + 1, other_lon)

    beside = jnp.where(lat > 0, 2, 0) + jnp.where(lat < lat_size - 1, 2, 0)
    pl.semaphore_wait(barrier, bits + beside)

    def row_copy(pair, f, up):
        src, dst = (rows, 0) if up else (1, rows + 1)
        return pltpu.make_async_remote_copy(
            src_ref=z.at[2 * pair + f, :, src, :, mid],
            dst_ref=z.at[2 * pair + f, :, dst, :, mid],
            send_sem=r["row_send"].at[pair, f, int(up)],
            recv_sem=r["row_recv"].at[pair, f, int(up)],
            device_id=(lat + 1 if up else lat - 1, lon),
            device_id_type=MESH,
        )

    def col_copy(pair, side, place):
        to_lat = (lat, lat + 1, lat - 1)[place]
        return pltpu.make_async_remote_copy(
            src_ref=r["rim_out"].at[pair, side],
            dst_ref=r["rim_in"].at[pair, side, place],
            send_sem=r["col_send"].at[pair, side, place],
            recv_sem=r["col_recv"].at[pair, side, place],
            device_id=(to_lat, other_lon),
            device_id_type=MESH,
        )

    def both_ways(up_copies, down_copies, what, mirrored):
        @pl.when(lat < lat_size - 1)
        def _():
            for c in down_copies if mirrored else up_copies:
                getattr(c, what)()

        @pl.when(lat > 0)
        def _():
            for c in up_copies if mirrored else down_copies:
                getattr(c, what)()

    def copies(pair):
        ups = [row_copy(pair, f, True) for f in range(2)] + [col_copy(pair, s, 1) for s in range(2)]
        downs = [row_copy(pair, f, False) for f in range(2)] + [col_copy(pair, s, 2) for s in range(2)]
        return ups, downs, [col_copy(pair, s, 0) for s in range(2)]

    def send_halo(pair):
        for f in range(2):
            for side, lo, pick in ((1, 0, 0), (0, cols - 16, 15)):
                for b in range(batch):
                    for i in range(1, rows + 1):
                        block = z[2 * pair + f, b, i, lo : lo + 16, mid].astype(F32)
                        r["rim32"][f, side, 2 * i + b : 2 * i + b + 1, :] = block[pick : pick + 1]
        for f in range(2):
            for side in range(2):
                r["rim_out"][pair, side, f] = r["rim32"][f, side].astype(BF16)
        ups, downs, flats = copies(pair)
        for c in flats:
            c.start()
        both_ways(ups, downs, "start", False)

    def shift_rows(pair, row_list):
        for f in range(2):
            fld = 2 * pair + f
            for b in range(batch):
                for i in row_list:
                    x = z[fld, b, i, :, mid].astype(F32)
                    z[fld, b, i, :, 0:chans] = pltpu.roll(x, 1, 0).astype(BF16)
                    z[fld, b, i, :, 2 * chans :] = pltpu.roll(x, cols - 1, 0).astype(BF16)

    def receive_halo(pair):
        ups, downs, flats = copies(pair)
        for c in flats:
            c.wait_recv()
        both_ways(ups, downs, "wait_recv", True)
        zero_row = jnp.zeros((batch, cols, chans), BF16)

        @pl.when(lat == 0)
        def _():
            for f in range(2):
                z[2 * pair + f, :, 0, :, mid] = zero_row
                for s in range(2):
                    r["rim_in"][pair, s, 1, f] = jnp.zeros((n_stage, chans), BF16)

        @pl.when(lat == lat_size - 1)
        def _():
            for f in range(2):
                z[2 * pair + f, :, rows + 1, :, mid] = zero_row
                for s in range(2):
                    r["rim_in"][pair, s, 2, f] = jnp.zeros((n_stage, chans), BF16)

        at = lax.broadcasted_iota(jnp.int32, (n_stage, chans), 0)
        for f in range(2):
            for s in range(2):
                centre = r["rim_in"][pair, s, 0, f].astype(F32)
                above = pltpu.roll(r["rim_in"][pair, s, 1, f].astype(F32), 4, 0)
                below = pltpu.roll(r["rim_in"][pair, s, 2, f].astype(F32), n_stage - 4, 0)
                r["rim32"][f, s] = jnp.where(at < 2, above, jnp.where(at >= n_stage - 2, below, centre))
        shift_rows(pair, (0, rows + 1))
        first = lax.broadcasted_iota(jnp.int32, (16, chans), 0) == 0
        final = lax.broadcasted_iota(jnp.int32, (16, chans), 0) == 15
        for f in range(2):
            fld = 2 * pair + f
            for b in range(batch):
                for i in range(padded_rows):
                    k = 2 * i + b
                    old = z[fld, b, i, 0:16, 0:chans].astype(F32)
                    z[fld, b, i, 0:16, 0:chans] = jnp.where(first, r["rim32"][f, 0, k : k + 1], old).astype(BF16)
                    old = z[fld, b, i, cols - 16 :, 2 * chans :].astype(F32)
                    z[fld, b, i, cols - 16 :, 2 * chans :] = jnp.where(
                        final, r["rim32"][f, 1, k : k + 1], old
                    ).astype(BF16)

    def finish_halo(pair):
        ups, downs, flats = copies(pair)
        for c in flats:
            c.wait_send()
        both_ways(ups, downs, "wait_send", False)

    def stage_copy(grp, s, p):
        op = plans[grp][s][0]
        to = (lat, other_lon) if op == "lon" else (partner(op), lon)
        return pltpu.make_async_remote_copy(
            src_ref=r[f"send{grp}{s}"].at[p],
            dst_ref=r[f"recv{grp}{s}"].at[p],
            send_sem=r["rs_send"].at[grp, s, p],
            recv_sem=r["rs_recv"].at[grp, s, p],
            device_id=to,
            device_id_type=MESH,
        )

    def half(grp, s, p, mine):
        op, length, width = plans[grp][s]
        keep = r[f"keep{grp}{s}"]
        if op == "lon":
            start = pl.multiple_of((lon if mine else other_lon) * (width // 2), width // 2)
            return keep[p, :, :, :, pl.ds(start, width // 2)]
        which = bit_of(op) if mine else 1 - bit_of(op)
        return keep[p, :, :, which]

    def put(grp, s, p, value):
        keep = r[f"keep{grp}{s}"]
        keep[p] = value.reshape(keep.shape[1:])
        r[f"send{grp}{s}"][p] = half(grp, s, p, False).astype(BF16)
        stage_copy(grp, s, p).start()

    def advance(grp, s, p):
        stage_copy(grp, s, p).wait_recv()
        value = half(grp, s, p, True) + r[f"recv{grp}{s}"][p].astype(F32)
        if s + 1 < len(plans[grp]):
            put(grp, s + 1, p, value)
            return
        value = (value * scale).reshape(3, value.shape[2], value.shape[3])
        e = p
        if grp == 0:
            for f in range(3):
                r["g2"][8 - 3 * e - f] = value[f]
        else:
            r["g1"][3 * e : 3 * e + 3] = value

    def window(fld, e):
        return z[fld, :, e : e + rows].reshape(batch * rows * cols, 3 * chans)

    def conv(fld, w, b):
        total = None
        for e in range(3):
            x = z[fld, b, e : e + rows].reshape(rows * cols, 3 * chans)
            part = jnp.dot(x, w[3 * e : 3 * e + 3].reshape(3 * chans, chans), preferred_element_type=F32)
            total = part if total is None else total + part
        return total

    loads[0].wait()
    loads[1].wait()
    send_halo(0)
    shift_rows(0, range(1, rows + 1))
    loads[2].wait()
    loads[3].wait()
    for t in range(9):
        r["w1t"][8 - t] = r["w1"][t].T
        r["w2t"][8 - t] = r["w2"][t].T
    receive_halo(0)

    for b in range(batch):
        pre = conv(0, r["w1"], b)
        sigma = 1.0 / (1.0 + jnp.exp(-pre))
        active = (pre * sigma).astype(BF16)
        z[2, b, 1 : rows + 1, :, mid] = active.reshape(rows, cols, chans)
        r["slope"][b] = sigma * (1.0 + pre * (1.0 - sigma))
    act = z[2, :, 1 : rows + 1, :, mid].reshape(batch * rows * cols, chans)
    for e in range(3):
        terms = lax.dot_general(act, window(1, e), (((0,), (0,)), ((), ())), preferred_element_type=F32)
        put(0, 0, e, jnp.stack([terms[:, f * chans : (f + 1) * chans] for f in range(3)]))
    for b in range(batch):
        back = (conv(1, r["w2t"], b) * r["slope"][b]).astype(BF16)
        z[3, b, 1 : rows + 1, :, mid] = back.reshape(rows, cols, chans)
    send_halo(1)
    for e in range(3):
        advance(0, 0, e)
    back = z[3, :, 1 : rows + 1, :, mid].reshape(batch * rows * cols, chans)
    for e in range(3):
        terms = lax.dot_general(window(0, e), back, (((0,), (0,)), ((), ())), preferred_element_type=F32)
        put(1, 0, e, terms)
    for e in range(3):
        advance(1, 0, e)
    shift_rows(1, range(1, rows + 1))
    receive_halo(1)
    for e in range(3):
        advance(0, 1, e)
    for b in range(batch):
        total = z[0, b, 1 : rows + 1, :, mid].astype(F32) + conv(2, r["w2"], b).reshape(rows, cols, chans)
        r["out"][b] = total.astype(BF16)
    for e in range(3):
        advance(1, 1, e)
    for b in range(batch):
        total = z[1, b, 1 : rows + 1, :, mid].astype(F32) + conv(3, r["w1t"], b).reshape(rows, cols, chans)
        r["sgrad"][b] = total.astype(BF16)
    for s in range(2, len(plans[0])):
        for grp in range(2):
            for e in range(3):
                advance(grp, s, e)
    for pair in range(2):
        finish_halo(pair)
    for grp in range(2):
        for s in range(len(plans[grp])):
            for e in range(3):
                stage_copy(grp, s, e).wait_send()


def fused_body(state, upstream, first_kernel, second_kernel):
    lat_size, lon_size = lax.axis_size("lat"), lax.axis_size("lon")
    batch, rows, cols, chans = state.shape
    scale = 1.0 / math.sqrt(rows * lat_size * cols * lon_size)
    own = chans // lat_size
    n_stage = 2 * (rows + 2)
    plans = [stage_plan(lat_size, chans, True), stage_plan(lat_size, chans, False)]
    steps = len(plans[0])
    scratch = {
        "z": pltpu.VMEM((4, batch, rows + 2, cols, 3 * chans), BF16),
        "w1": pltpu.VMEM((9, chans, chans), BF16),
        "w2": pltpu.VMEM((9, chans, chans), BF16),
        "w1t": pltpu.VMEM((9, chans, chans), BF16),
        "w2t": pltpu.VMEM((9, chans, chans), BF16),
        "slope": pltpu.VMEM((batch, rows * cols, chans), F32),
        "rim32": pltpu.VMEM((2, 2, n_stage, chans), F32),
        "rim_out": pltpu.VMEM((2, 2, 2, n_stage, chans), BF16),
        "rim_in": pltpu.VMEM((2, 2, 3, 2, n_stage, chans), BF16),
        "load_sem": pltpu.SemaphoreType.DMA((4,)),
        "row_send": pltpu.SemaphoreType.DMA((2, 2, 2)),
        "row_recv": pltpu.SemaphoreType.DMA((2, 2, 2)),
        "col_send": pltpu.SemaphoreType.DMA((2, 2, 3)),
        "col_recv": pltpu.SemaphoreType.DMA((2, 2, 3)),
        "rs_send": pltpu.SemaphoreType.DMA((2, steps, 3)),
        "rs_recv": pltpu.SemaphoreType.DMA((2, steps, 3)),
    }
    for grp in range(2):
        for s, (op, length, width) in enumerate(plans[grp]):
            if op == "lon":
                kept, sent = (3, length, own, width), (3, length, own, width // 2)
            else:
                kept, sent = (3, length // 2, 2, own, width), (3, length // 2, own, width)
            scratch[f"keep{grp}{s}"] = pltpu.VMEM((3,) + kept, F32)
            scratch[f"send{grp}{s}"] = pltpu.VMEM((3,) + sent, BF16)
            scratch[f"recv{grp}{s}"] = pltpu.VMEM((3,) + sent, BF16)
    names = ["state", "upstream", "k1", "k2", "out", "sgrad", "g1", "g2"] + list(scratch)

    def kernel(*refs):
        fused_kernel(lat_size, scale, plans, names, *refs)

    vmem = pl.BlockSpec(memory_space=pltpu.VMEM)
    return pl.pallas_call(
        kernel,
        out_shape=(
            jax.ShapeDtypeStruct(state.shape, BF16),
            jax.ShapeDtypeStruct(state.shape, BF16),
            jax.ShapeDtypeStruct((9, own, chans // 2), F32),
            jax.ShapeDtypeStruct((9, own, chans // 2), F32),
        ),
        in_specs=[pl.BlockSpec(memory_space=pl.ANY)] * 4,
        out_specs=(vmem,) * 4,
        scratch_shapes=list(scratch.values()),
        compiler_params=pltpu.CompilerParams(
            collective_id=0, has_side_effects=True, vmem_limit_bytes=56 * 2**20
        ),
    )(state, upstream, first_kernel, second_kernel)


def body(state, upstream, first_kernel, second_kernel):
    lat_size, lon_size = lax.axis_size("lat"), lax.axis_size("lon")
    batch, rows, cols, chans = state.shape
    fits = (
        lon_size == 2
        and lat_size >= 4
        and lat_size & (lat_size - 1) == 0
        and batch == 2
        and 2 * (rows + 2) == 16
        and cols % 16 == 0
        and chans % (16 * lat_size) == 0
        and (chans // 2) % 128 == 0
    )
    run = fused_body if fits else general_body
    return run(state, upstream, first_kernel, second_kernel)


def solution(mesh):
    placed = (P(None, "lat", "lon", None), P(None, "lat", "lon", None), P(), P())
    return jax.shard_map(
        body,
        mesh=mesh,
        in_specs=placed,
        out_specs=(
            P(None, "lat", "lon", None),
            P(None, "lat", "lon", None),
            P(None, "lat", "lon"),
            P(None, "lat", "lon"),
        ),
        check_vma=False,
    )
```

time: 194 us -> 44.8 us (0.23)
  the two profiles are of different devices: /device:TPU:20 before, /device:TPU:0 now
where the time goes in v1:
time: 44.8 us; the launch traced here: 44.6 us
  Pallas kernels  39.1 us (87%)
  local copies, waits for them, and re-layouts  4.84 us (11%)
  between operations  0.66 us (1%)
    pallas_call x1, Pallas kernels, fused_body(): pl.pallas_call(kernel, out_shape=(jax.ShapeDtypeStruct(state.shape, BF16)...  39.1 us
    unnamed x8, local copies, waits for them, and re-layouts  4.84 us

profile of v1, /device:TPU:0, one launch (start us, length us, event | category | flops | bytes accessed | tf_op | source)
XLA Modules:
  0.0 44.6 jit_solution(10906785010830928568)
XLA Ops:
  0.6 39.1 %shard_map.75 = (bf16[2,6,64,256]{3,2,1,0:T(8,128)(2,1)}, bf16[2,6,64,256]{3,2,1,0:T(8,128)(2,1)}, f32[9,16,128]{2,1,0:T(8,128)}, f32[9,16,128]{2,1,0:T(8,128)}) custom-call(bf16[2,6,64,256]{3,2,1,0:T(8,128)(2,1)} %refs_0_.1, bf16[2,6,64,256]{3,2,1,0:T(8,128)(2,1)} %refs_1_.1, bf16[9,256,256]{2,1,0:T(8,128)(2,1)} %refs_2_.1, bf16[9,256,256]{2,1,0:T(8,128)(2,1)} %refs_3_.1), custom_call_target="tpu_custom_call" | custom-call | tf_op jit(solution)/shard_map/pallas_call | solution.py:406
  39.8 0.0 copy-start.1
  39.8 0.0 copy-start
  39.8 1.8 %copy.12 = bf16[2,6,64,256]{3,2,1,0:T(8,128)(2,1)} copy(bf16[2,6,64,256]{3,2,1,0:T(8,128)(2,1)} %get-tuple-element.8) | data formatting | bytes 786432
  41.6 1.8 %copy.13 = bf16[2,6,64,256]{3,2,1,0:T(8,128)(2,1)} copy(bf16[2,6,64,256]{3,2,1,0:T(8,128)(2,1)} %get-tuple-element.9) | data formatting | bytes 786432
  43.4 0.0 copy-done.1
  43.4 0.6 %copy.14 = f32[9,16,128]{2,1,0:T(8,128)} copy(f32[9,16,128]{2,1,0:T(8,128)S(1)} %copy-done.1) | data formatting | bytes 147456
  44.0 0.0 copy-done
  44.0 0.6 %copy.15 = f32[9,16,128]{2,1,0:T(8,128)} copy(f32[9,16,128]{2,1,0:T(8,128)S(1)} %copy-done) | data formatting | bytes 147456
Async XLA Ops:
  39.8 3.6 %copy-start.1 = (f32[9,16,128]{2,1,0:T(8,128)S(1)}, f32[9,16,128]{2,1,0:T(8,128)}, u32[]{:S(2)}) copy-start(f32[9,16,128]{2,1,0:T(8,128)} %get-tuple-element.10) | copy-start | bytes 221188
  39.8 4.2 %copy-start = (f32[9,16,128]{2,1,0:T(8,128)S(1)}, f32[9,16,128]{2,1,0:T(8,128)}, u32[]{:S(2)}) copy-start(f32[9,16,128]{2,1,0:T(8,128)} %get-tuple-element.11) | copy-start | bytes 221188

commit v2 on v1

--- a/solution.py
+++ b/solution.py
@@ -93,6 +93,10 @@
     return plan
 
 
+PIECES = (((2, 0), (2, 2), (1, 1)), ((2, 1), (1, 0), (1, 2)))
+ORDER = ((0, 0), (1, 0), (0, 1), (1, 1), (0, 2), (1, 2))
+
+
 def fused_kernel(lat_size, scale, plans, names, *refs):
     r = dict(zip(names, refs))
     z = r["z"]
@@ -153,14 +157,23 @@
             device_id_type=MESH,
         )
 
-    def col_copy(pair, side, place):
-        to_lat = (lat, lat + 1, lat - 1)[place]
+    def rim_copy(pair):
         return pltpu.make_async_remote_copy(
-            src_ref=r["rim_out"].at[pair, side],
-            dst_ref=r["rim_in"].at[pair, side, place],
-            send_sem=r["col_send"].at[pair, side, place],
-            recv_sem=r["col_recv"].at[pair, side, place],
-            device_id=(to_lat, other_lon),
+            src_ref=r["rim_out"].at[pair],
+            dst_ref=r["rim_in"].at[pair],
+            send_sem=r["rim_send"].at[pair],
+            recv_sem=r["rim_recv"].at[pair],
+            device_id=(lat, other_lon),
+            device_id_type=MESH,
+        )
+
+    def corner_copy(pair, up):
+        return pltpu.make_async_remote_copy(
+            src_ref=r["corner_out"].at[pair, int(up)],
+            dst_ref=r["corner_in"].at[pair, int(up)],
+            send_sem=r["corner_send"].at[pair, int(up)],
+            recv_sem=r["corner_recv"].at[pair, int(up)],
+            device_id=(lat + 1 if up else lat - 1, other_lon),
             device_id_type=MESH,
         )
 
@@ -176,9 +189,9 @@
                 getattr(c, what)()
 
     def copies(pair):
-        ups = [row_copy(pair, f, True) for f in range(2)] + [col_copy(pair, s, 1) for s in range(2)]
-        downs = [row_copy(pair, f, False) for f in range(2)] + [col_copy(pair, s, 2) for s in range(2)]
-        return ups, downs, [col_copy(pair, s, 0) for s in range(2)]
+        ups = [corner_copy(pair, True)] + [row_copy(pair, f, True) for f in range(2)]
+        downs = [corner_copy(pair, False)] + [row_copy(pair, f, False) for f in range(2)]
+        return ups, downs, [rim_copy(pair)]
 
     def send_halo(pair):
         for f in range(2):
@@ -190,6 +203,11 @@
         for f in range(2):
             for side in range(2):
                 r["rim_out"][pair, side, f] = r["rim32"][f, side].astype(BF16)
+                k = 2 * (2 * side + f)
+                r["corner32"][0, k : k + 2] = r["rim32"][f, side, 2:4]
+                r["corner32"][1, k : k + 2] = r["rim32"][f, side, n_stage - 4 : n_stage - 2]
+        for up in range(2):
+            r["corner_out"][pair, up] = r["corner32"][up].astype(BF16)
         ups, downs, flats = copies(pair)
         for c in flats:
             c.start()
@@ -213,25 +231,24 @@
 
         @pl.when(lat == 0)
         def _():
+            r["corner_in"][pair, 1] = jnp.zeros((16, chans), BF16)
             for f in range(2):
                 z[2 * pair + f, :, 0, :, mid] = zero_row
-                for s in range(2):
-                    r["rim_in"][pair, s, 1, f] = jnp.zeros((n_stage, chans), BF16)
 
         @pl.when(lat == lat_size - 1)
         def _():
+            r["corner_in"][pair, 0] = jnp.zeros((16, chans), BF16)
             for f in range(2):
                 z[2 * pair + f, :, rows + 1, :, mid] = zero_row
-                for s in range(2):
-                    r["rim_in"][pair, s, 2, f] = jnp.zeros((n_stage, chans), BF16)
-
-        at = lax.broadcasted_iota(jnp.int32, (n_stage, chans), 0)
+
+        for up in range(2):
+            r["corner32"][up] = r["corner_in"][pair, up].astype(F32)
         for f in range(2):
             for s in range(2):
-                centre = r["rim_in"][pair, s, 0, f].astype(F32)
-                above = pltpu.roll(r["rim_in"][pair, s, 1, f].astype(F32), 4, 0)
-                below = pltpu.roll(r["rim_in"][pair, s, 2, f].astype(F32), n_stage - 4, 0)
-                r["rim32"][f, s] = jnp.where(at < 2, above, jnp.where(at >= n_stage - 2, below, centre))
+                k = 2 * (2 * s + f)
+                r["rim32"][f, s] = r["rim_in"][pair, s, f].astype(F32)
+                r["rim32"][f, s, 0:2] = r["corner32"][1, k : k + 2]
+                r["rim32"][f, s, n_stage - 2 :] = r["corner32"][0, k : k + 2]
         shift_rows(pair, (0, rows + 1))
         first = lax.broadcasted_iota(jnp.int32, (16, chans), 0) == 0
         final = lax.broadcasted_iota(jnp.int32, (16, chans), 0) == 15
@@ -287,8 +304,8 @@
             put(grp, s + 1, p, value)
             return
         value = (value * scale).reshape(3, value.shape[2], value.shape[3])
-        e = p
-        if grp == 0:
+        grad, e = PIECES[grp][p]
+        if grad == 2:
             for f in range(3):
                 r["g2"][8 - 3 * e - f] = value[f]
         else:
@@ -325,35 +342,43 @@
     act = z[2, :, 1 : rows + 1, :, mid].reshape(batch * rows * cols, chans)
     for e in range(3):
         terms = lax.dot_general(act, window(1, e), (((0,), (0,)), ((), ())), preferred_element_type=F32)
-        put(0, 0, e, jnp.stack([terms[:, f * chans : (f + 1) * chans] for f in range(3)]))
+        grp, p = ORDER[e]
+        put(grp, 0, p, jnp.stack([terms[:, f * chans : (f + 1) * chans] for f in range(3)]))
     for b in range(batch):
         back = (conv(1, r["w2t"], b) * r["slope"][b]).astype(BF16)
         z[3, b, 1 : rows + 1, :, mid] = back.reshape(rows, cols, chans)
     send_halo(1)
-    for e in range(3):
-        advance(0, 0, e)
+
+    def advance_all(s, pieces):
+        for grp, p in pieces:
+            advance(grp, s, p)
+
+    early, late = ORDER[:3], ORDER[3:]
+    advance_all(0, early)
     back = z[3, :, 1 : rows + 1, :, mid].reshape(batch * rows * cols, chans)
     for e in range(3):
         terms = lax.dot_general(window(0, e), back, (((0,), (0,)), ((), ())), preferred_element_type=F32)
-        put(1, 0, e, terms)
-    for e in range(3):
-        advance(1, 0, e)
+        grp, p = late[e]
+        put(grp, 0, p, terms)
+    advance_all(0, late)
+    advance_all(1, early)
     shift_rows(1, range(1, rows + 1))
     receive_halo(1)
-    for e in range(3):
-        advance(0, 1, e)
-    for b in range(batch):
-        total = z[0, b, 1 : rows + 1, :, mid].astype(F32) + conv(2, r["w2"], b).reshape(rows, cols, chans)
-        r["out"][b] = total.astype(BF16)
-    for e in range(3):
-        advance(1, 1, e)
-    for b in range(batch):
-        total = z[1, b, 1 : rows + 1, :, mid].astype(F32) + conv(3, r["w1t"], b).reshape(rows, cols, chans)
-        r["sgrad"][b] = total.astype(BF16)
-    for s in range(2, len(plans[0])):
-        for grp in range(2):
-            for e in range(3):
-                advance(grp, s, e)
+
+    def finish_field(fld, w, name, b):
+        near = z[fld, b, 1 : rows + 1, :, mid].astype(F32)
+        r[name][b] = (near + conv(fld + 2, w, b).reshape(rows, cols, chans)).astype(BF16)
+
+    finish_field(0, r["w2"], "out", 0)
+    advance_all(1, late)
+    finish_field(0, r["w2"], "out", 1)
+    advance_all(2, early)
+    finish_field(1, r["w1t"], "sgrad", 0)
+    advance_all(2, late)
+    finish_field(1, r["w1t"], "sgrad", 1)
+    for s in range(3, len(plans[0])):
+        advance_all(s, early)
+        advance_all(s, late)
     for pair in range(2):
         finish_halo(pair)
     for grp in range(2):
@@ -379,12 +404,17 @@
         "slope": pltpu.VMEM((batch, rows * cols, chans), F32),
         "rim32": pltpu.VMEM((2, 2, n_stage, chans), F32),
         "rim_out": pltpu.VMEM((2, 2, 2, n_stage, chans), BF16),
-        "rim_in": pltpu.VMEM((2, 2, 3, 2, n_stage, chans), BF16),
+        "rim_in": pltpu.VMEM((2, 2, 2, n_stage, chans), BF16),
+        "corner32": pltpu.VMEM((2, 16, chans), F32),
+        "corner_out": pltpu.VMEM((2, 2, 16, chans), BF16),
+        "corner_in": pltpu.VMEM((2, 2, 16, chans), BF16),
         "load_sem": pltpu.SemaphoreType.DMA((4,)),
         "row_send": pltpu.SemaphoreType.DMA((2, 2, 2)),
         "row_recv": pltpu.SemaphoreType.DMA((2, 2, 2)),
-        "col_send": pltpu.SemaphoreType.DMA((2, 2, 3)),
-        "col_recv": pltpu.SemaphoreType.DMA((2, 2, 3)),
+        "rim_send": pltpu.SemaphoreType.DMA((2,)),
+        "rim_recv": pltpu.SemaphoreType.DMA((2,)),
+        "corner_send": pltpu.SemaphoreType.DMA((2, 2)),
+        "corner_recv": pltpu.SemaphoreType.DMA((2, 2)),
         "rs_send": pltpu.SemaphoreType.DMA((2, steps, 3)),
         "rs_recv": pltpu.SemaphoreType.DMA((2, steps, 3)),
     }
@@ -403,21 +433,33 @@
         fused_kernel(lat_size, scale, plans, names, *refs)
 
     vmem = pl.BlockSpec(memory_space=pltpu.VMEM)
-    return pl.pallas_call(
+    anywhere = pl.BlockSpec(memory_space=pltpu.HBM)
+    kinds = [(state.shape, BF16)] * 2 + [((9, own, chans // 2), F32)] * 2
+    held = pl.pallas_call(
         kernel,
-        out_shape=(
-            jax.ShapeDtypeStruct(state.shape, BF16),
-            jax.ShapeDtypeStruct(state.shape, BF16),
-            jax.ShapeDtypeStruct((9, own, chans // 2), F32),
-            jax.ShapeDtypeStruct((9, own, chans // 2), F32),
-        ),
-        in_specs=[pl.BlockSpec(memory_space=pl.ANY)] * 4,
+        out_shape=tuple(pltpu.VMEM(shape, kind) for shape, kind in kinds),
+        in_specs=[anywhere] * 4,
         out_specs=(vmem,) * 4,
         scratch_shapes=list(scratch.values()),
         compiler_params=pltpu.CompilerParams(
-            collective_id=0, has_side_effects=True, vmem_limit_bytes=56 * 2**20
+            collective_id=0, has_side_effects=True, vmem_limit_bytes=52 * 2**20
         ),
     )(state, upstream, first_kernel, second_kernel)
+
+    def write_out(*refs):
+        moves = [pltpu.make_async_copy(refs[i], refs[4 + i], refs[8].at[i]) for i in range(4)]
+        for move in moves:
+            move.start()
+        for move in moves:
+            move.wait()
+
+    return pl.pallas_call(
+        write_out,
+        out_shape=tuple(jax.ShapeDtypeStruct(shape, kind) for shape, kind in kinds),
+        in_specs=[vmem] * 4,
+        out_specs=(anywhere,) * 4,
+        scratch_shapes=[pltpu.SemaphoreType.DMA((4,))],
+    )(*[pltpu.with_memory_space_constraint(h, pltpu.VMEM) for h in held])
 
 
 def body(state, upstream, first_kernel, second_kernel):

time: 44.8 us -> 39.5 us (0.88)
  local copies, waits for them, and re-layouts: 4.84 us -> 1.98 us
  Pallas kernels: 39.1 us -> 36.6 us
    unnamed x8 -> x4, local copies, waits for them, and re-layouts: 4.84 us -> 1.98 us
    pallas_call x1 -> x2, Pallas kernels: 39.1 us -> 36.6 us  [the longest x1 35.7 us: fused_body(): pl.pallas_call(kernel, out_shape=tuple((pltpu.VMEM(shape, kind) for shape...]
where the time goes in v2:
time: 39.5 us; the launch traced here: 39.3 us
  Pallas kernels  36.6 us (93%)
  local copies, waits for them, and re-layouts  1.98 us (5%)
  between operations  0.65 us (2%)
    pallas_call x1, Pallas kernels, fused_body(): pl.pallas_call(kernel, out_shape=tuple((pltpu.VMEM(shape, kind) for shape...  35.7 us
    unnamed x4, local copies, waits for them, and re-layouts  1.98 us
    pallas_call x1, Pallas kernels, fused_body(): pl.pallas_call(write_out, out_shape=tuple((jax.ShapeDtypeStruct(shape, ki...  0.95 us

profile of v2, /device:TPU:0, one launch (start us, length us, event | category | flops | bytes accessed | tf_op | source)
XLA Modules:
  0.0 39.3 jit_solution(17526066956707484961)
XLA Ops:
  0.6 0.0 copy-start
  0.6 1.0 %copy-done = bf16[2,6,64,256]{3,2,1,0:T(8,128)(2,1)S(1)} copy-done((bf16[2,6,64,256]{3,2,1,0:T(8,128)(2,1)S(1)}, bf16[2,6,64,256]{3,2,1,0:T(8,128)(2,1)}, u32[]{:S(2)}) %copy-start) | copy-done | bytes 393240
  1.6 0.0 copy-start.1
  1.6 1.0 %copy-done.1 = bf16[2,6,64,256]{3,2,1,0:T(8,128)(2,1)S(1)} copy-done((bf16[2,6,64,256]{3,2,1,0:T(8,128)(2,1)S(1)}, bf16[2,6,64,256]{3,2,1,0:T(8,128)(2,1)}, u32[]{:S(2)}) %copy-start.1) | copy-done | bytes 393240
  2.6 35.7 %shard_map.75 = (bf16[2,6,64,256]{3,2,1,0:T(8,128)(2,1)S(1)}, bf16[2,6,64,256]{3,2,1,0:T(8,128)(2,1)S(1)}, f32[9,16,128]{2,1,0:T(8,128)S(1)}, f32[9,16,128]{2,1,0:T(8,128)S(1)}) custom-call(bf16[2,6,64,256]{3,2,1,0:T(8,128)(2,1)S(1)} %copy-done, bf16[2,6,64,256]{3,2,1,0:T(8,128)(2,1)S(1)} %copy-done.1, bf16[9,256,256]{2,1,0:T(8,128)(2,1)} %refs_2_.1, ...), custom_call_target="tpu_custom_call" | custom-call | tf_op jit(solution)/shard_map/pallas_call | solution.py:438
  38.3 1.0 %shard_map.76 = (bf16[2,6,64,256]{3,2,1,0:T(8,128)(2,1)}, bf16[2,6,64,256]{3,2,1,0:T(8,128)(2,1)}, f32[9,16,128]{2,1,0:T(8,128)}, f32[9,16,128]{2,1,0:T(8,128)}) custom-call(bf16[2,6,64,256]{3,2,1,0:T(8,128)(2,1)S(1)} %get-tuple-element.8.refs_0_, bf16[2,6,64,256]{3,2,1,0:T(8,128)(2,1)S(1)} %get-tuple-element.9.refs_1_, ...), custom_call_target="tpu_custom_call" | custom-call | tf_op jit(solution)/shard_map/pallas_call | solution.py:456
Async XLA Ops:
  0.6 1.0 %copy-start = (bf16[2,6,64,256]{3,2,1,0:T(8,128)(2,1)S(1)}, bf16[2,6,64,256]{3,2,1,0:T(8,128)(2,1)}, u32[]{:S(2)}) copy-start(bf16[2,6,64,256]{3,2,1,0:T(8,128)(2,1)} %refs_0_.1) | copy-start | bytes 1179652
  1.6 1.0 %copy-start.1 = (bf16[2,6,64,256]{3,2,1,0:T(8,128)(2,1)S(1)}, bf16[2,6,64,256]{3,2,1,0:T(8,128)(2,1)}, u32[]{:S(2)}) copy-start(bf16[2,6,64,256]{3,2,1,0:T(8,128)(2,1)} %refs_1_.1) | copy-start | bytes 1179652

commit v3 on v2

--- a/solution.py
+++ b/solution.py
@@ -79,22 +79,26 @@
     return (output_state, state_grad, summed[0], summed[1])
 
 
-def stage_plan(lat_size, chans, lon_first):
+def stage_plan(lat_size, chans, first):
     bits = lat_size.bit_length() - 1
-    order = [0, "lon", 1] if lon_first else [0, 1, "lon"]
-    order += list(range(2, bits))
-    plan, length, cols = [], lat_size, chans
+    turns = [["lon"], [1], list(range(2, bits))]
+    order = [0]
+    for turn in (turns, turns[1:] + turns[:1], turns[2:] + turns[:2])[first]:
+        order += turn
+    left, plan, cols = list(range(bits)), [], chans
     for op in order:
-        plan.append((op, length, cols))
         if op == "lon":
+            plan.append((op, 2 ** len(left), 1, cols))
             cols //= 2
         else:
-            length //= 2
+            at = left.index(op)
+            plan.append((op, 2 ** (len(left) - 1 - at), 2**at, cols))
+            left.remove(op)
     return plan
 
 
-PIECES = (((2, 0), (2, 2), (1, 1)), ((2, 1), (1, 0), (1, 2)))
-ORDER = ((0, 0), (1, 0), (0, 1), (1, 1), (0, 2), (1, 2))
+PIECES = (((2, 0), (1, 0)), ((2, 1), (1, 1)), ((2, 2), (1, 2)))
+ORDER = ((0, 0), (1, 0), (2, 0), (0, 1), (1, 1), (2, 1))
 
 
 def fused_kernel(lat_size, scale, plans, names, *refs):
@@ -283,11 +287,11 @@
         )
 
     def half(grp, s, p, mine):
-        op, length, width = plans[grp][s]
+        op, _, _, width = plans[grp][s]
         keep = r[f"keep{grp}{s}"]
         if op == "lon":
             start = pl.multiple_of((lon if mine else other_lon) * (width // 2), width // 2)
-            return keep[p, :, :, :, pl.ds(start, width // 2)]
+            return keep[p, :, :, :, :, pl.ds(start, width // 2)]
         which = bit_of(op) if mine else 1 - bit_of(op)
         return keep[p, :, :, which]
 
@@ -303,7 +307,7 @@
         if s + 1 < len(plans[grp]):
             put(grp, s + 1, p, value)
             return
-        value = (value * scale).reshape(3, value.shape[2], value.shape[3])
+        value = (value * scale).reshape(3, value.shape[-2], value.shape[-1])
         grad, e = PIECES[grp][p]
         if grad == 2:
             for f in range(3):
@@ -344,47 +348,50 @@
         terms = lax.dot_general(act, window(1, e), (((0,), (0,)), ((), ())), preferred_element_type=F32)
         grp, p = ORDER[e]
         put(grp, 0, p, jnp.stack([terms[:, f * chans : (f + 1) * chans] for f in range(3)]))
+    early, late = ORDER[:3], ORDER[3:]
+
+    def advance_all(s, pieces):
+        for grp, p in pieces:
+            advance(grp, s, p)
+
     for b in range(batch):
         back = (conv(1, r["w2t"], b) * r["slope"][b]).astype(BF16)
         z[3, b, 1 : rows + 1, :, mid] = back.reshape(rows, cols, chans)
-    send_halo(1)
-
-    def advance_all(s, pieces):
-        for grp, p in pieces:
-            advance(grp, s, p)
-
-    early, late = ORDER[:3], ORDER[3:]
-    advance_all(0, early)
+        if b == 0:
+            advance_all(0, early)
     back = z[3, :, 1 : rows + 1, :, mid].reshape(batch * rows * cols, chans)
     for e in range(3):
         terms = lax.dot_general(window(0, e), back, (((0,), (0,)), ((), ())), preferred_element_type=F32)
         grp, p = late[e]
         put(grp, 0, p, terms)
+    send_halo(1)
     advance_all(0, late)
     advance_all(1, early)
     shift_rows(1, range(1, rows + 1))
+    advance_all(1, late)
     receive_halo(1)
+    advance_all(2, early)
 
     def finish_field(fld, w, name, b):
         near = z[fld, b, 1 : rows + 1, :, mid].astype(F32)
         r[name][b] = (near + conv(fld + 2, w, b).reshape(rows, cols, chans)).astype(BF16)
 
     finish_field(0, r["w2"], "out", 0)
-    advance_all(1, late)
+    advance_all(2, late)
     finish_field(0, r["w2"], "out", 1)
-    advance_all(2, early)
+    advance_all(3, early)
     finish_field(1, r["w1t"], "sgrad", 0)
-    advance_all(2, late)
+    advance_all(3, late)
     finish_field(1, r["w1t"], "sgrad", 1)
-    for s in range(3, len(plans[0])):
+    for s in range(4, len(plans[0])):
         advance_all(s, early)
         advance_all(s, late)
     for pair in range(2):
         finish_halo(pair)
-    for grp in range(2):
+    for grp in range(3):
         for s in range(len(plans[grp])):
-            for e in range(3):
-                stage_copy(grp, s, e).wait_send()
+            for p in range(2):
+                stage_copy(grp, s, p).wait_send()
 
 
 def fused_body(state, upstream, first_kernel, second_kernel):
@@ -393,7 +400,7 @@
     scale = 1.0 / math.sqrt(rows * lat_size * cols * lon_size)
     own = chans // lat_size
     n_stage = 2 * (rows + 2)
-    plans = [stage_plan(lat_size, chans, True), stage_plan(lat_size, chans, False)]
+    plans = [stage_plan(lat_size, chans, first) for first in range(3)]
     steps = len(plans[0])
     scratch = {
         "z": pltpu.VMEM((4, batch, rows + 2, cols, 3 * chans), BF16),
@@ -415,18 +422,18 @@
         "rim_recv": pltpu.SemaphoreType.DMA((2,)),
         "corner_send": pltpu.SemaphoreType.DMA((2, 2)),
         "corner_recv": pltpu.SemaphoreType.DMA((2, 2)),
-        "rs_send": pltpu.SemaphoreType.DMA((2, steps, 3)),
-        "rs_recv": pltpu.SemaphoreType.DMA((2, steps, 3)),
+        "rs_send": pltpu.SemaphoreType.DMA((3, steps, 2)),
+        "rs_recv": pltpu.SemaphoreType.DMA((3, steps, 2)),
     }
-    for grp in range(2):
-        for s, (op, length, width) in enumerate(plans[grp]):
+    for grp in range(3):
+        for s, (op, high, low, width) in enumerate(plans[grp]):
             if op == "lon":
-                kept, sent = (3, length, own, width), (3, length, own, width // 2)
+                kept, sent = (2, 3, high, low, own, width), (2, 3, high, low, own, width // 2)
             else:
-                kept, sent = (3, length // 2, 2, own, width), (3, length // 2, own, width)
-            scratch[f"keep{grp}{s}"] = pltpu.VMEM((3,) + kept, F32)
-            scratch[f"send{grp}{s}"] = pltpu.VMEM((3,) + sent, BF16)
-            scratch[f"recv{grp}{s}"] = pltpu.VMEM((3,) + sent, BF16)
+                kept, sent = (2, 3, high, 2, low, own, width), (2, 3, high, low, own, width)
+            scratch[f"keep{grp}{s}"] = pltpu.VMEM(kept, F32)
+            scratch[f"send{grp}{s}"] = pltpu.VMEM(sent, BF16)
+            scratch[f"recv{grp}{s}"] = pltpu.VMEM(sent, BF16)
     names = ["state", "upstream", "k1", "k2", "out", "sgrad", "g1", "g2"] + list(scratch)
 
     def kernel(*refs):
@@ -442,9 +449,9 @@
         out_specs=(vmem,) * 4,
         scratch_shapes=list(scratch.values()),
         compiler_params=pltpu.CompilerParams(
-            collective_id=0, has_side_effects=True, vmem_limit_bytes=52 * 2**20
+            collective_id=0, has_side_effects=True, vmem_limit_bytes=56 * 2**20
         ),
-    )(state, upstream, first_kernel, second_kernel)
+    )(*[pltpu.with_memory_space_constraint(x, pltpu.HBM) for x in (state, upstream, first_kernel, second_kernel)])
 
     def write_out(*refs):
         moves = [pltpu.make_async_copy(refs[i], refs[4 + i], refs[8].at[i]) for i in range(4)]
@@ -467,7 +474,7 @@
     batch, rows, cols, chans = state.shape
     fits = (
         lon_size == 2
-        and lat_size >= 4
+        and lat_size >= 16
         and lat_size & (lat_size - 1) == 0
         and batch == 2
         and 2 * (rows + 2) == 16

time: 39.5 us -> 38 us (0.962)
  local copies, waits for them, and re-layouts: 1.98 us -> 0 us
  Pallas kernels: 36.6 us -> 37.2 us
    unnamed x4 -> x0, local copies, waits for them, and re-layouts: 1.98 us -> none
    pallas_call x1, Pallas kernels: 35.7 us -> 36.2 us  [fused_body(): pl.pallas_call(kernel, out_shape=tuple((pltpu.VMEM(shape, kind) for shape...]
where the time goes in v3:
time: 38 us; the launch traced here: 37.8 us
  Pallas kernels  37.2 us (98%)
  between operations  0.64 us (2%)
    pallas_call x1, Pallas kernels, fused_body(): pl.pallas_call(kernel, out_shape=tuple((pltpu.VMEM(shape, kind) for shape...  36.2 us
    pallas_call x1, Pallas kernels, fused_body(): pl.pallas_call(write_out, out_shape=tuple((jax.ShapeDtypeStruct(shape, ki...  0.95 us

profile of v3, /device:TPU:0, one launch (start us, length us, event | category | flops | bytes accessed | tf_op | source)
XLA Modules:
  0.0 37.8 jit_solution(6033530666153865879)
XLA Ops:
  0.6 36.2 %shard_map.75 = (bf16[2,6,64,256]{3,2,1,0:T(8,128)(2,1)S(1)}, bf16[2,6,64,256]{3,2,1,0:T(8,128)(2,1)S(1)}, f32[9,16,128]{2,1,0:T(8,128)S(1)}, f32[9,16,128]{2,1,0:T(8,128)S(1)}) custom-call(bf16[2,6,64,256]{3,2,1,0:T(8,128)(2,1)} %refs_0_.1, bf16[2,6,64,256]{3,2,1,0:T(8,128)(2,1)} %refs_1_.1, bf16[9,256,256]{2,1,0:T(8,128)(2,1)} %refs_2_.1, ...), custom_call_target="tpu_custom_call" | custom-call | tf_op jit(solution)/shard_map/pallas_call | solution.py:445
  36.9 1.0 %shard_map.76 = (bf16[2,6,64,256]{3,2,1,0:T(8,128)(2,1)}, bf16[2,6,64,256]{3,2,1,0:T(8,128)(2,1)}, f32[9,16,128]{2,1,0:T(8,128)}, f32[9,16,128]{2,1,0:T(8,128)}) custom-call(bf16[2,6,64,256]{3,2,1,0:T(8,128)(2,1)S(1)} %get-tuple-element.8.refs_0_, bf16[2,6,64,256]{3,2,1,0:T(8,128)(2,1)S(1)} %get-tuple-element.9.refs_1_, ...), custom_call_target="tpu_custom_call" | custom-call | tf_op jit(solution)/shard_map/pallas_call | solution.py:463

commit v4 on v3

--- a/solution.py
+++ b/solution.py
@@ -198,6 +198,8 @@
         return ups, downs, [rim_copy(pair)]
 
     def send_halo(pair):
+        ups, downs, flats = copies(pair)
+        both_ways(ups[1:], downs[1:], "start", False)
         for f in range(2):
             for side, lo, pick in ((1, 0, 0), (0, cols - 16, 15)):
                 for b in range(batch):
@@ -212,10 +214,9 @@
                 r["corner32"][1, k : k + 2] = r["rim32"][f, side, n_stage - 4 : n_stage - 2]
         for up in range(2):
             r["corner_out"][pair, up] = r["corner32"][up].astype(BF16)
-        ups, downs, flats = copies(pair)
         for c in flats:
             c.start()
-        both_ways(ups, downs, "start", False)
+        both_ways(ups[:1], downs[:1], "start", False)
 
     def shift_rows(pair, row_list):
         for f in range(2):
@@ -333,7 +334,6 @@
     loads[2].wait()
     loads[3].wait()
     for t in range(9):
-        r["w1t"][8 - t] = r["w1"][t].T
         r["w2t"][8 - t] = r["w2"][t].T
     receive_halo(0)
 
@@ -368,6 +368,8 @@
     advance_all(0, late)
     advance_all(1, early)
     shift_rows(1, range(1, rows + 1))
+    for t in range(9):
+        r["w1t"][8 - t] = r["w1"][t].T
     advance_all(1, late)
     receive_halo(1)
     advance_all(2, early)

time: 38 us -> 38.9 us (1.024)
  Pallas kernels: 37.2 us -> 38.1 us
    pallas_call x1, Pallas kernels: 36.2 us -> 37.1 us  [fused_body(): pl.pallas_call(kernel, out_shape=tuple((pltpu.VMEM(shape, kind) for shape...]
where the time goes in v4:
time: 38.9 us; the launch traced here: 38.7 us
  Pallas kernels  38.1 us (98%)
  between operations  0.64 us (2%)
    pallas_call x1, Pallas kernels, fused_body(): pl.pallas_call(kernel, out_shape=tuple((pltpu.VMEM(shape, kind) for shape...  37.1 us
    pallas_call x1, Pallas kernels, fused_body(): pl.pallas_call(write_out, out_shape=tuple((jax.ShapeDtypeStruct(shape, ki...  0.95 us

profile of v4, /device:TPU:0, one launch (start us, length us, event | category | flops | bytes accessed | tf_op | source)
XLA Modules:
  0.0 38.7 jit_solution(11549869174865356982)
XLA Ops:
  0.6 37.1 %shard_map.75 = (bf16[2,6,64,256]{3,2,1,0:T(8,128)(2,1)S(1)}, bf16[2,6,64,256]{3,2,1,0:T(8,128)(2,1)S(1)}, f32[9,16,128]{2,1,0:T(8,128)S(1)}, f32[9,16,128]{2,1,0:T(8,128)S(1)}) custom-call(bf16[2,6,64,256]{3,2,1,0:T(8,128)(2,1)} %refs_0_.1, bf16[2,6,64,256]{3,2,1,0:T(8,128)(2,1)} %refs_1_.1, bf16[9,256,256]{2,1,0:T(8,128)(2,1)} %refs_2_.1, ...), custom_call_target="tpu_custom_call" | custom-call | tf_op jit(solution)/shard_map/pallas_call | solution.py:447
  37.8 1.0 %shard_map.76 = (bf16[2,6,64,256]{3,2,1,0:T(8,128)(2,1)}, bf16[2,6,64,256]{3,2,1,0:T(8,128)(2,1)}, f32[9,16,128]{2,1,0:T(8,128)}, f32[9,16,128]{2,1,0:T(8,128)}) custom-call(bf16[2,6,64,256]{3,2,1,0:T(8,128)(2,1)S(1)} %get-tuple-element.8.refs_0_, bf16[2,6,64,256]{3,2,1,0:T(8,128)(2,1)S(1)} %get-tuple-element.9.refs_1_, ...), custom_call_target="tpu_custom_call" | custom-call | tf_op jit(solution)/shard_map/pallas_call | solution.py:465

commit v5 on v2

--- a/solution.py
+++ b/solution.py
@@ -442,9 +442,9 @@
         out_specs=(vmem,) * 4,
         scratch_shapes=list(scratch.values()),
         compiler_params=pltpu.CompilerParams(
-            collective_id=0, has_side_effects=True, vmem_limit_bytes=52 * 2**20
+            collective_id=0, has_side_effects=True, vmem_limit_bytes=56 * 2**20
         ),
-    )(state, upstream, first_kernel, second_kernel)
+    )(*[pltpu.with_memory_space_constraint(x, pltpu.HBM) for x in (state, upstream, first_kernel, second_kernel)])
 
     def write_out(*refs):
         moves = [pltpu.make_async_copy(refs[i], refs[4 + i], refs[8].at[i]) for i in range(4)]

time: 39.5 us -> 37.4 us (0.947)
  local copies, waits for them, and re-layouts: 1.98 us -> 0 us
    unnamed x4 -> x0, local copies, waits for them, and re-layouts: 1.98 us -> none
where the time goes in v5:
time: 37.4 us; the launch traced here: 37.3 us
  Pallas kernels  36.6 us (98%)
  between operations  0.64 us (2%)
    pallas_call x1, Pallas kernels, fused_body(): pl.pallas_call(kernel, out_shape=tuple((pltpu.VMEM(shape, kind) for shape...  35.7 us
    pallas_call x1, Pallas kernels, fused_body(): pl.pallas_call(write_out, out_shape=tuple((jax.ShapeDtypeStruct(shape, ki...  0.95 us

profile of v5, /device:TPU:0, one launch (start us, length us, event | category | flops | bytes accessed | tf_op | source)
XLA Modules:
  0.0 37.3 jit_solution(8375640940853210567)
XLA Ops:
  0.6 35.7 %shard_map.75 = (bf16[2,6,64,256]{3,2,1,0:T(8,128)(2,1)S(1)}, bf16[2,6,64,256]{3,2,1,0:T(8,128)(2,1)S(1)}, f32[9,16,128]{2,1,0:T(8,128)S(1)}, f32[9,16,128]{2,1,0:T(8,128)S(1)}) custom-call(bf16[2,6,64,256]{3,2,1,0:T(8,128)(2,1)} %refs_0_.1, bf16[2,6,64,256]{3,2,1,0:T(8,128)(2,1)} %refs_1_.1, bf16[9,256,256]{2,1,0:T(8,128)(2,1)} %refs_2_.1, ...), custom_call_target="tpu_custom_call" | custom-call | tf_op jit(solution)/shard_map/pallas_call | solution.py:438
  36.3 1.0 %shard_map.76 = (bf16[2,6,64,256]{3,2,1,0:T(8,128)(2,1)}, bf16[2,6,64,256]{3,2,1,0:T(8,128)(2,1)}, f32[9,16,128]{2,1,0:T(8,128)}, f32[9,16,128]{2,1,0:T(8,128)}) custom-call(bf16[2,6,64,256]{3,2,1,0:T(8,128)(2,1)S(1)} %get-tuple-element.8.refs_0_, bf16[2,6,64,256]{3,2,1,0:T(8,128)(2,1)S(1)} %get-tuple-element.9.refs_1_, ...), custom_call_target="tpu_custom_call" | custom-call | tf_op jit(solution)/shard_map/pallas_call | solution.py:456
